TPU v7x, 32 devices: a whole 2x2x4 slice. The times are simulated.
32 devices in a mesh: expert: 8 (over y, x, core), replica: 4 (over z).
Axes of the slice: x: 2, y: 2, z: 4, core: 2. Of those that a mesh axis runs over, the one named last changes fastest.
Arguments:
- tokens: bfloat16 [16384, 2048], P(('expert', 'replica')), may hold values from -6 to 6
- d_hidden: bfloat16 [16384, 768], P(('expert', 'replica')), may hold values from -6 to 6
- w_gate: bfloat16 [32, 2048, 768], P(None, ('expert', 'replica')), may hold values from -0.125 to 0.125
- w_up: bfloat16 [32, 2048, 768], P(None, ('expert', 'replica')), may hold values from -0.125 to 0.125
- expert_ids: int32 [32], replicated, may hold values from 0 to 31
Outputs:
- hidden: bfloat16 [16384, 768], P(('expert', 'replica'))
- token_grad: bfloat16 [16384, 2048], P(('expert', 'replica'))
- grad_gate: bfloat16 [32, 2048, 768], P(None, ('expert', 'replica'))
- grad_up: bfloat16 [32, 2048, 768], P(None, ('expert', 'replica'))
Inputs may be any that keep to these rules, and one draw needn't show every extreme that they name: expert_ids[b] is the expert used by the rows of block b; several blocks may use the same expert.
All inputs are finite; a program needn't handle non-finite values.
Results may differ from a plain program's by a relative error of at most 0.0057.
Values may be sent and summed in bfloat16 or wider, within the bound.
A program may use at most 128 MiB of HBM per device.

v0:
```python
import jax
import jax.numpy as jnp
from jax import lax
from jax.sharding import PartitionSpec as P


def pick_pieces(weights, chosen, leading):
    return jnp.take(weights, chosen, axis=0).reshape(leading + weights.shape[1:])


def per_device(tokens, d_hidden, w_gate, w_up, expert_ids):
    owner_count = lax.axis_size("expert")
    member_count = lax.axis_size("replica")
    block_rows = w_gate.shape[1]
    hidden_width = w_gate.shape[2]
    model_width = owner_count * member_count * block_rows
    reordered = expert_ids.reshape(owner_count, member_count).T.reshape(-1)
    leading = (member_count, owner_count)
    outgoing = (pick_pieces(w_gate, reordered, leading), pick_pieces(w_up, reordered, leading))
    gate_parts, up_parts = (
        lax.all_to_all(
            lax.all_to_all(outgoing[0], "replica", split_axis=0, concat_axis=0, tiled=True),
            "expert",
            split_axis=1,
            concat_axis=0,
            tiled=True,
        ),
        lax.all_to_all(
            lax.all_to_all(outgoing[1], "replica", split_axis=0, concat_axis=0, tiled=True),
            "expert",
            split_axis=1,
            concat_axis=0,
            tiled=True,
        ),
    )
    gate_whole = gate_parts.reshape(model_width, hidden_width)
    up_whole = up_parts.reshape(model_width, hidden_width)
    gate_pre = jnp.dot(tokens, gate_whole, preferred_element_type=jnp.float32)
    up_pre = jnp.dot(tokens, up_whole, preferred_element_type=jnp.float32)
    sigmoid_gate = jax.nn.sigmoid(gate_pre)
    activated = gate_pre * sigmoid_gate
    hidden = (activated * up_pre).astype(jnp.bfloat16)
    upstream = d_hidden.astype(jnp.float32)
    d_gate = (upstream * up_pre * sigmoid_gate * (1.0 + gate_pre * (1.0 - sigmoid_gate))).astype(
        jnp.bfloat16
    )
    d_up = (upstream * activated).astype(jnp.bfloat16)
    back_dims = (((1,), (1,)), ((), ()))
    token_grad = (
        lax.dot_general(d_gate, gate_whole, back_dims, preferred_element_type=jnp.float32)
        + lax.dot_general(d_up, up_whole, back_dims, preferred_element_type=jnp.float32)
    ).astype(jnp.bfloat16)
    outer_dims = (((0,), (0,)), ((), ()))
    shape_parts = (owner_count, member_count, block_rows, hidden_width)
    part_gate = (
        lax.dot_general(tokens, d_gate, outer_dims, preferred_element_type=jnp.float32)
        .astype(jnp.bfloat16)
        .reshape(shape_parts)
    )
    part_up = (
        lax.dot_general(tokens, d_up, outer_dims, preferred_element_type=jnp.float32)
        .astype(jnp.bfloat16)
        .reshape(shape_parts)
    )
    gate_terms, up_terms = (
        lax.all_to_all(
            lax.all_to_all(part_gate, "expert", split_axis=0, concat_axis=0, tiled=True),
            "replica",
            split_axis=1,
            concat_axis=1,
            tiled=True,
        ),
        lax.all_to_all(
            lax.all_to_all(part_up, "expert", split_axis=0, concat_axis=0, tiled=True),
            "replica",
            split_axis=1,
            concat_axis=1,
            tiled=True,
        ),
    )
    block_count = owner_count * member_count
    expert_total = w_gate.shape[0]
    selector = (expert_ids[None, :] == jnp.arange(expert_total, dtype=jnp.int32)[:, None]).astype(
        jnp.bfloat16
    )
    scale = tokens.shape[0] ** (-0.5)
    flat_gate = gate_terms.reshape(block_count, block_rows * hidden_width)
    flat_up = up_terms.reshape(block_count, block_rows * hidden_width)
    grad_gate = (
        (jnp.dot(selector, flat_gate, preferred_element_type=jnp.float32) * scale)
        .reshape(expert_total, block_rows, hidden_width)
        .astype(jnp.bfloat16)
    )
    grad_up = (
        (jnp.dot(selector, flat_up, preferred_element_type=jnp.float32) * scale)
        .reshape(expert_total, block_rows, hidden_width)
        .astype(jnp.bfloat16)
    )
    return (hidden, token_grad, grad_gate, grad_up)


def solution(mesh):
    in_specs = (
        P(("expert", "replica"), None),
        P(("expert", "replica"), None),
        P(None, ("expert", "replica"), None),
        P(None, ("expert", "replica"), None),
        P(),
    )
    out_specs = (
        P(("expert", "replica"), None),
        P(("expert", "replica"), None),
        P(None, ("expert", "replica"), None),
        P(None, ("expert", "replica"), None),
    )
    return jax.shard_map(
        per_device, mesh=mesh, in_specs=in_specs, out_specs=out_specs, check_vma=False
    )
```

profile of v0, /device:TPU:24, one launch (start us, length us, event | category | flops | bytes accessed | tf_op | source)
XLA Modules:
  0.0 482.3 jit_solution(2120658771893733739)
XLA Ops:
  5.0 4.4 gather_fusion
  9.4 4.2 broadcast_select_fusion.1
  13.6 73.5 %all_to_all.60 = bf16[4,8,64,768]{3,2,1,0:T(8,128)(2,1)} all-to-all(bf16[4,8,64,768]{3,2,1,0:T(8,128)(2,1)S(1)} %bitcast.79), channel_id=1, replica_groups=mesh['expert'=8,'replica'=4] {'replica'}, dimensions={0} | all-to-all | bytes 6291456 | tf_op jit(solution)/shard_map/all_to_all | solution.py:22
  87.1 5.8 %all-to-all-start.2 = ((bf16[4,8,64,768]{3,2,1,0:T(8,128)(2,1)}), bf16[4,8,64,768]{3,2,1,0:T(8,128)(2,1)S(1)}, u32[]{:S(2)}, u32[]{:S(2)}) async-start(bf16[4,8,64,768]{3,2,1,0:T(8,128)(2,1)} %bitcast.78), calls=%async_computation.2 | async-start | bytes 6291456 | tf_op jit(solution)/shard_map/all_to_all | solution.py:29
  92.9 3.9 copy.25
  96.8 63.6 %all-to-all-done.2 = bf16[4,8,64,768]{3,2,1,0:T(8,128)(2,1)S(1)} async-done(((bf16[4,8,64,768]{3,2,1,0:T(8,128)(2,1)}), bf16[4,8,64,768]{3,2,1,0:T(8,128)(2,1)S(1)}, u32[]{:S(2)}, u32[]{:S(2)}) %all-to-all-start.2) | async-done | bytes 3145760 | tf_op jit(solution)/shard_map/all_to_all | solution.py:29
  160.4 4.5 all-to-all-start.1
  166.9 35.9 %all-to-all-done.1 = bf16[4,8,64,768]{3,2,0,1:T(8,128)(2,1)} async-done(((bf16[4,8,64,768]{3,2,0,1:T(8,128)(2,1)}), bf16[4,8,64,768]{3,2,0,1:T(8,128)(2,1)}, u32[]{:S(2)}, u32[]{:S(2)}) %all-to-all-start.1) | async-done | bytes 3145760 | tf_op jit(solution)/shard_map/all_to_all | solution.py:21
  202.7 3.7 all-to-all-start.3
  208.8 4.5 fusion.17
  218.0 4.7 copy.31
  222.6 21.6 %all-to-all-done.3 = bf16[4,8,64,768]{3,2,0,1:T(8,128)(2,1)S(1)} async-done(((bf16[4,8,64,768]{3,2,0,1:T(8,128)(2,1)}), bf16[4,8,64,768]{3,2,0,1:T(8,128)(2,1)S(1)}, u32[]{:S(2)}, u32[]{:S(2)}) %all-to-all-start.3) | async-done | bytes 3145760 | tf_op jit(solution)/shard_map/all_to_all | solution.py:28
  245.9 3.6 all-to-all-start.6
  249.5 6.5 %fusion.6 = (bf16[512,768]{0,1:T(8,128)(2,1)S(1)}, bf16[512,768]{0,1:T(8,128)(2,1)}) fusion(bf16[512,768]{0,1:T(8,128)(2,1)} %copy.27, f32[768,512]{1,0:T(8,128)} %copy-done.13, bf16[2048,768]{1,0:T(8,128)(2,1)} %bitcast.80, bf16[512,2048]{1,0:T(8,128)(2,1)} %param.7), kind=kOutput, calls=%fused_computation.17 | convolution fusion | flops 1616117760 | bytes 9175040 | tf_op jit(solution)/shard_map/dot_general | solution.py:39
  260.4 4.7 copy.28
  265.1 22.2 %all-to-all-done.6 = bf16[8,4,64,768]{3,2,1,0:T(8,128)(2,1)S(1)} async-done(((bf16[8,4,64,768]{3,2,1,0:T(8,128)(2,1)}), bf16[8,4,64,768]{3,2,1,0:T(8,128)(2,1)S(1)}, u32[]{:S(2)}, u32[]{:S(2)}) %all-to-all-start.6) | async-done | bytes 3145760 | tf_op jit(solution)/shard_map/all_to_all | solution.py:74
  287.3 4.5 all-to-all-start.4
  293.8 35.9 %all-to-all-done.4 = bf16[8,4,64,768]{3,2,1,0:T(8,128)(2,1)} async-done(((bf16[8,4,64,768]{3,2,1,0:T(8,128)(2,1)}), bf16[8,4,64,768]{3,2,1,0:T(8,128)(2,1)}, u32[]{:S(2)}, u32[]{:S(2)}) %all-to-all-start.4) | async-done | bytes 3145760 | tf_op jit(solution)/shard_map/all_to_all | solution.py:67
  329.6 6.0 %all-to-all-start.7 = ((bf16[8,4,64,768]{3,2,0,1:T(8,128)(2,1)}), bf16[8,4,64,768]{3,2,0,1:T(8,128)(2,1)S(1)}, u32[]{:S(2)}, u32[]{:S(2)}) async-start(bf16[8,4,64,768]{3,2,0,1:T(8,128)(2,1)} %copy.32), calls=%async_computation.7 | async-start | bytes 6291456 | tf_op jit(solution)/shard_map/all_to_all | solution.py:73
  335.7 3.9 copy.29
  339.5 61.8 %all-to-all-done.7 = bf16[8,4,64,768]{3,2,0,1:T(8,128)(2,1)S(1)} async-done(((bf16[8,4,64,768]{3,2,0,1:T(8,128)(2,1)}), bf16[8,4,64,768]{3,2,0,1:T(8,128)(2,1)S(1)}, u32[]{:S(2)}, u32[]{:S(2)}) %all-to-all-start.7) | async-done | bytes 3145760 | tf_op jit(solution)/shard_map/all_to_all | solution.py:73
  403.0 6.0 %all-to-all-start.5 = ((bf16[8,4,64,768]{3,2,0,1:T(8,128)(2,1)}), bf16[8,4,64,768]{3,2,0,1:T(8,128)(2,1)S(1)}, u32[]{:S(2)}, u32[]{:S(2)}) async-start(bf16[8,4,64,768]{3,2,0,1:T(8,128)(2,1)} %copy.29), calls=%async_computation.5 | async-start | bytes 6291456 | tf_op jit(solution)/shard_map/all_to_all | solution.py:66
  411.3 4.1 fusion.18
  424.1 52.8 %all-to-all-done.5 = bf16[8,4,64,768]{3,2,0,1:T(8,128)(2,1)S(1)} async-done(((bf16[8,4,64,768]{3,2,0,1:T(8,128)(2,1)}), bf16[8,4,64,768]{3,2,0,1:T(8,128)(2,1)S(1)}, u32[]{:S(2)}, u32[]{:S(2)}) %all-to-all-start.5) | async-done | bytes 3145760 | tf_op jit(solution)/shard_map/all_to_all | solution.py:66
  (52 shorter events, 39.3 us)
Async XLA Ops:
  0.6 1.9 copy-start
  5.0 4.5 copy-start.4
  87.1 73.3 %all-to-all-start.2 = ((bf16[4,8,64,768]{3,2,1,0:T(8,128)(2,1)}), bf16[4,8,64,768]{3,2,1,0:T(8,128)(2,1)S(1)}, u32[]{:S(2)}, u32[]{:S(2)}) async-start(bf16[4,8,64,768]{3,2,1,0:T(8,128)(2,1)} %bitcast.78), calls=%async_computation.2 | async-start | bytes 6291456 | tf_op jit(solution)/shard_map/all_to_all | solution.py:29
  160.4 42.3 %all-to-all-start.1 = ((bf16[4,8,64,768]{3,2,0,1:T(8,128)(2,1)}), bf16[4,8,64,768]{3,2,0,1:T(8,128)(2,1)}, u32[]{:S(2)}, u32[]{:S(2)}) async-start(bf16[4,8,64,768]{3,2,0,1:T(8,128)(2,1)} %copy.25), calls=%async_computation.1 | async-start | bytes 6291456 | tf_op jit(solution)/shard_map/all_to_all | solution.py:21
  202.7 41.4 %all-to-all-start.3 = ((bf16[4,8,64,768]{3,2,0,1:T(8,128)(2,1)}), bf16[4,8,64,768]{3,2,0,1:T(8,128)(2,1)S(1)}, u32[]{:S(2)}, u32[]{:S(2)}) async-start(bf16[4,8,64,768]{3,2,0,1:T(8,128)(2,1)} %copy.26), calls=%async_computation.3 | async-start | bytes 6291456 | tf_op jit(solution)/shard_map/all_to_all | solution.py:28
  208.8 5.7 %copy-start.7 = (bf16[512,768]{0,1:T(8,128)(2,1)S(1)}, bf16[512,768]{0,1:T(8,128)(2,1)}, u32[]{:S(2)}) copy-start(bf16[512,768]{0,1:T(8,128)(2,1)} %copy.27) | copy-start | bytes 2359300
  208.8 5.7 %copy-start.10 = (bf16[512,2048]{1,0:T(8,128)(2,1)S(1)}, bf16[512,2048]{1,0:T(8,128)(2,1)}, u32[]{:S(2)}) copy-start(bf16[512,2048]{1,0:T(8,128)(2,1)} %param.7) | copy-start | bytes 6291460
  213.3 1.1 copy-start.13
  244.2 1.7 copy-start.5
  245.9 41.4 %all-to-all-start.6 = ((bf16[8,4,64,768]{3,2,1,0:T(8,128)(2,1)}), bf16[8,4,64,768]{3,2,1,0:T(8,128)(2,1)S(1)}, u32[]{:S(2)}, u32[]{:S(2)}) async-start(bf16[8,4,64,768]{3,2,1,0:T(8,128)(2,1)} %bitcast.70), calls=%async_computation.6 | async-start | bytes 6291456 | tf_op jit(solution)/shard_map/all_to_all | solution.py:74
  249.5 7.4 %copy-start.11 = (bf16[512,2048]{1,0:T(8,128)(2,1)S(1)}, bf16[512,2048]{1,0:T(8,128)(2,1)}, u32[]{:S(2)}) copy-start(bf16[512,2048]{1,0:T(8,128)(2,1)} %param.7) | copy-start | bytes 6291460
  256.1 0.9 copy-start.12
  287.3 42.3 %all-to-all-start.4 = ((bf16[8,4,64,768]{3,2,1,0:T(8,128)(2,1)}), bf16[8,4,64,768]{3,2,1,0:T(8,128)(2,1)}, u32[]{:S(2)}, u32[]{:S(2)}) async-start(bf16[8,4,64,768]{3,2,1,0:T(8,128)(2,1)} %bitcast.71), calls=%async_computation.4 | async-start | bytes 6291456 | tf_op jit(solution)/shard_map/all_to_all | solution.py:67
  329.6 71.7 %all-to-all-start.7 = ((bf16[8,4,64,768]{3,2,0,1:T(8,128)(2,1)}), bf16[8,4,64,768]{3,2,0,1:T(8,128)(2,1)S(1)}, u32[]{:S(2)}, u32[]{:S(2)}) async-start(bf16[8,4,64,768]{3,2,0,1:T(8,128)(2,1)} %copy.32), calls=%async_computation.7 | async-start | bytes 6291456 | tf_op jit(solution)/shard_map/all_to_all | solution.py:73
  401.3 1.7 copy-start.2
  403.0 73.9 %all-to-all-start.5 = ((bf16[8,4,64,768]{3,2,0,1:T(8,128)(2,1)}), bf16[8,4,64,768]{3,2,0,1:T(8,128)(2,1)S(1)}, u32[]{:S(2)}, u32[]{:S(2)}) async-start(bf16[8,4,64,768]{3,2,0,1:T(8,128)(2,1)} %copy.29), calls=%async_computation.5 | async-start | bytes 6291456 | tf_op jit(solution)/shard_map/all_to_all | solution.py:66
  411.3 4.1 copy-start.6
  411.3 4.1 copy-start.8
  411.3 4.2 copy-start.14
  415.5 3.3 copy-start.3
  419.0 1.8 copy-start.9
  479.9 2.4 copy-start.1
where the time goes:
time: 488 us; the launch traced here: 482 us
  waiting for transfers between devices  294 us (60%)
  blocking collectives  73.5 us (15%)
  local copies, waits for them, and re-layouts  48.6 us (10%)
  starting transfers between devices  34.1 us (7%)
  matrix products  27.4 us (6%)
    all_to_all x1, blocking collectives, per_device(): lax.all_to_all(outgoing[0], 'replica', split_axis=0, concat_axis=0, tiled...  73.5 us
    all_to_all x1, waiting for transfers between devices, per_device(): lax.all_to_all(outgoing[1], 'replica', split_axis=0, concat_axis=0, tiled...  63.6 us
    all_to_all x1, waiting for transfers between devices, per_device(): lax.all_to_all(lax.all_to_all(part_up, 'expert', split_axis=0, concat_axi...  61.8 us
    all_to_all x1, waiting for transfers between devices, per_device(): lax.all_to_all(lax.all_to_all(part_gate, 'expert', split_axis=0, concat_a...  52.8 us
    all_to_all x1, waiting for transfers between devices, per_device(): lax.all_to_all(lax.all_to_all(outgoing[0], 'replica', split_axis=0, conca...  35.9 us
    all_to_all x1, waiting for transfers between devices, per_device(): lax.all_to_all(part_gate, 'expert', split_axis=0, concat_axis=0, tiled=True)  35.9 us
    all_to_all x1, waiting for transfers between devices, per_device(): lax.all_to_all(part_up, 'expert', split_axis=0, concat_axis=0, tiled=True)  22.2 us
    all_to_all x1, waiting for transfers between devices, per_device(): lax.all_to_all(lax.all_to_all(outgoing[1], 'replica', split_axis=0, conca...  21.6 us
  transfers between devices with their start and end apart: 7, of which 7 were waited for; matrix products, arithmetic and copies ran while one was open for 12% of the time, Pallas kernels for 0%

commit v1 on v0

v1 whole, which is shorter than its diff:
```python
import functools

import jax
import jax.numpy as jnp
from jax import lax
from jax.experimental import pallas as pl
from jax.experimental.pallas import tpu as pltpu
from jax.sharding import PartitionSpec as P

MESH = pl.DeviceIdType.MESH
ANY = pl.BlockSpec(memory_space=pl.ANY)
BF16 = jnp.bfloat16
F32 = jnp.float32


def chunk_count(width):
    for chunks in (3, 2):
        if width % (chunks * 128) == 0:
            return chunks
    return 1


def pick_kernel(step_blocks, chunks, ids_ref, gate_ref, up_ref, out_ref, sem):
    first = pl.program_id(0) * step_blocks
    width = out_ref.shape[3] // 2
    copies = []
    for i in range(step_blocks):
        which = ids_ref[first + i]
        for c in range(chunks):
            for half, source in enumerate((gate_ref, up_ref)):
                copies.append(
                    pltpu.make_async_copy(
                        source.at[which, :, pl.ds(c * width, width)],
                        out_ref.at[c, i, :, pl.ds(half * width, width)],
                        sem.at[i, c, half],
                    )
                )
    for copy in copies:
        copy.start()
    for copy in copies:
        copy.wait()


def pick(w_gate, w_up, expert_ids, chunks):
    blocks = expert_ids.shape[0]
    _, rows, hidden = w_gate.shape
    both = 2 * hidden // chunks
    step_blocks = 8
    return pl.pallas_call(
        functools.partial(pick_kernel, step_blocks, chunks),
        grid_spec=pltpu.PrefetchScalarGridSpec(
            num_scalar_prefetch=1,
            grid=(blocks // step_blocks,),
            in_specs=[ANY, ANY],
            out_specs=pl.BlockSpec(
                (chunks, step_blocks, rows, both), lambda s, ids: (0, s, 0, 0)
            ),
            scratch_shapes=[pltpu.SemaphoreType.DMA((step_blocks, chunks, 2))],
        ),
        out_shape=jax.ShapeDtypeStruct((chunks, blocks, rows, both), BF16),
    )(expert_ids, w_gate, w_up)


def main_kernel(
    owners,
    members,
    chunks,
    rows,
    tok_hbm,
    dh_hbm,
    out_w,
    hid_hbm,
    tg_hbm,
    terms,
    tok,
    tok_t,
    dh,
    hid,
    wbuf,
    part,
    dcat,
    acc,
    tg,
    load_sem,
    own_sem,
    w_send,
    w_recv,
    g_send,
    g_recv,
    out_sem,
):
    total = owners * members
    e = lax.axis_index("expert")
    z = lax.axis_index("replica")
    me = e * members + z
    tokens_n, model = tok.shape
    both = wbuf.shape[3]
    width = both // 2
    half = members // 2

    def partner(k):
        i = k // members
        j = (k % members + half) % members
        pe = (e + i) % owners
        pz = (z + j) % members
        return pe, pz, pe * members + pz

    def source_of(k):
        i = k // members
        j = (k % members + half) % members
        se = (e + owners - i) % owners
        sz = (z + members - j) % members
        return se, sz, se * members + sz

    def each_other(fn):
        @pl.loop(0, half)
        def _(k):
            fn(k)

        @pl.loop(half + 1, total)
        def _(k):
            fn(k)

    loads = [
        pltpu.make_async_copy(tok_hbm, tok, load_sem.at[0]),
        pltpu.make_async_copy(dh_hbm, dh, load_sem.at[1]),
    ]
    for copy in loads:
        copy.start()

    barrier = pltpu.get_barrier_semaphore()

    def greet(k):
        pe, pz, _ = partner(k)
        pl.semaphore_signal(barrier, inc=1, device_id=(pe, pz), device_id_type=MESH)

    each_other(greet)
    pl.semaphore_wait(barrier, total - 1)

    def w_copy(c, k):
        pe, pz, p = partner(k)
        return pltpu.make_async_remote_copy(
            src_ref=out_w.at[c, p],
            dst_ref=wbuf.at[c, me],
            send_sem=w_send.at[c, k],
            recv_sem=w_recv.at[c, k],
            device_id=(pe, pz),
            device_id_type=MESH,
        )

    def g_copy(c, k):
        pe, pz, p = partner(k)
        return pltpu.make_async_remote_copy(
            src_ref=part.at[c, p],
            dst_ref=terms.at[c, me],
            send_sem=g_send.at[c, k],
            recv_sem=g_recv.at[c, k],
            device_id=(pe, pz),
            device_id_type=MESH,
        )

    for c in range(chunks):
        each_other(lambda k, c=c: w_copy(c, k).start())
        pltpu.make_async_copy(out_w.at[c, me], wbuf.at[c, me], own_sem.at[0, c]).start()

    for copy in loads:
        copy.wait()
    tile = 256
    for r in range(model // tile):
        tok_t[r * tile : (r + 1) * tile, :] = tok[:, r * tile : (r + 1) * tile].T

    per_tile = tile // rows
    for c in range(chunks):
        cols = slice(c * width, (c + 1) * width)
        pltpu.make_async_copy(out_w.at[c, me], wbuf.at[c, me], own_sem.at[0, c]).wait()
        each_other(lambda k, c=c: w_copy(c, k).wait_recv())
        weights = wbuf.at[c]

        @pl.loop(0, tokens_n // tile)
        def _(r, c=c, cols=cols):
            at = pl.ds(pl.multiple_of(r * tile, tile), tile)
            pre = jnp.dot(
                tok[at, :],
                wbuf[c].reshape(model, both),
                preferred_element_type=F32,
            )
            gate, up = pre[:, :width], pre[:, width:]
            s = jax.nn.sigmoid(gate)
            activated = gate * s
            upstream = dh[at, cols].astype(F32)
            hid[at, cols] = (activated * up).astype(BF16)
            dcat[at, :width] = (upstream * up * s * (1.0 + gate * (1.0 - s))).astype(BF16)
            dcat[at, width:] = (upstream * activated).astype(BF16)

        @pl.loop(0, model // tile)
        def _(r, c=c):
            at = pl.ds(pl.multiple_of(r * tile, tile), tile)
            out = jnp.dot(tok_t[at, :], dcat[...], preferred_element_type=F32)
            part[c, pl.ds(r * per_tile, per_tile)] = out.astype(BF16).reshape(
                per_tile, rows, both
            )

        each_other(lambda k, c=c: g_copy(c, k).start())
        pltpu.make_async_copy(part.at[c, me], terms.at[c, me], own_sem.at[1, c]).start()

        @pl.loop(0, model // tile)
        def _(r, c=c):
            at = pl.ds(pl.multiple_of(r * tile, tile), tile)
            piece = wbuf[c, pl.ds(r * per_tile, per_tile)].reshape(tile, both)
            out = lax.dot_general(
                dcat[...], piece, (((1,), (1,)), ((), ())), preferred_element_type=F32
            )
            if c > 0:
                out = out + acc[r]
            if c == chunks - 1:
                tg[:, at] = out.astype(BF16)
            else:
                acc[r] = out

    outs = [
        pltpu.make_async_copy(hid, hid_hbm, out_sem.at[0]),
        pltpu.make_async_copy(tg, tg_hbm, out_sem.at[1]),
    ]
    for copy in outs:
        copy.start()
    for copy in outs:
        copy.wait()
    for c in range(chunks):
        each_other(lambda k, c=c: w_copy(c, k).wait_send())
        pltpu.make_async_copy(part.at[c, me], terms.at[c, me], own_sem.at[1, c]).wait()
        each_other(lambda k, c=c: g_copy(c, k).wait_send())
        each_other(lambda k, c=c: g_copy(c, k).wait_recv())


def exchange(tokens, d_hidden, out_w, owners, members):
    chunks, total, rows, both = out_w.shape
    tokens_n, model = tokens.shape
    hidden = d_hidden.shape[1]
    return pl.pallas_call(
        functools.partial(main_kernel, owners, members, chunks, rows),
        in_specs=[ANY, ANY, ANY],
        out_specs=[ANY, ANY, ANY],
        out_shape=[
            jax.ShapeDtypeStruct((tokens_n, hidden), BF16),
            jax.ShapeDtypeStruct((tokens_n, model), BF16),
            jax.ShapeDtypeStruct((chunks, total, rows, both), BF16),
        ],
        scratch_shapes=[
            pltpu.VMEM((tokens_n, model), BF16),
            pltpu.VMEM((model, tokens_n), BF16),
            pltpu.VMEM((tokens_n, hidden), BF16),
            pltpu.VMEM((tokens_n, hidden), BF16),
            pltpu.VMEM((chunks, total, rows, both), BF16),
            pltpu.VMEM((chunks, total, rows, both), BF16),
            pltpu.VMEM((tokens_n, both), BF16),
            pltpu.VMEM((model // 256, tokens_n, 256), F32),
            pltpu.VMEM((tokens_n, model), BF16),
            pltpu.SemaphoreType.DMA((2,)),
            pltpu.SemaphoreType.DMA((2, chunks)),
            pltpu.SemaphoreType.DMA((chunks, total)),
            pltpu.SemaphoreType.DMA((chunks, total)),
            pltpu.SemaphoreType.DMA((chunks, total)),
            pltpu.SemaphoreType.DMA((chunks, total)),
            pltpu.SemaphoreType.DMA((2,)),
        ],
        compiler_params=pltpu.CompilerParams(collective_id=0, has_side_effects=True),
    )(tokens, d_hidden, out_w)


def sum_kernel(scale, spread_ref, terms_ref, gate_ref, up_ref):
    _, blocks, group, both = terms_ref.shape
    experts = gate_ref.shape[0]
    width = both // 2
    flat = terms_ref[0].reshape(blocks * group, both)
    out = jnp.dot(spread_ref[...], flat, preferred_element_type=F32) * scale
    out = out.astype(BF16)
    gate_ref[...] = out[:, :width].reshape(experts, group, width)
    up_ref[...] = out[:, width:].reshape(experts, group, width)


def sum_terms(terms, expert_ids, experts, scale):
    chunks, blocks, rows, both = terms.shape
    width = both // 2
    group = min(rows, 16)
    selector = expert_ids[None, :] == jnp.arange(experts, dtype=jnp.int32)[:, None]
    unit = jnp.arange(group)[:, None] == jnp.arange(group)[None, :]
    spread = (selector[:, None, :, None] & unit[None, :, None, :]).astype(BF16)
    spread = spread.reshape(experts * group, blocks * group)
    result = jax.ShapeDtypeStruct((experts, rows, chunks * width), BF16)
    block = pl.BlockSpec((experts, group, width), lambda c, r: (0, r, c))
    return pl.pallas_call(
        functools.partial(sum_kernel, scale),
        grid=(chunks, rows // group),
        in_specs=[
            pl.BlockSpec((experts * group, blocks * group), lambda c, r: (0, 0)),
            pl.BlockSpec((1, blocks, group, both), lambda c, r: (c, 0, r, 0)),
        ],
        out_specs=[block, block],
        out_shape=[result, result],
    )(spread, terms)


def per_device(tokens, d_hidden, w_gate, w_up, expert_ids):
    owners = lax.axis_size("expert")
    members = lax.axis_size("replica")
    chunks = chunk_count(w_gate.shape[2])
    out_w = pick(w_gate, w_up, expert_ids, chunks)
    hidden, token_grad, terms = exchange(tokens, d_hidden, out_w, owners, members)
    scale = tokens.shape[0] ** (-0.5)
    grad_gate, grad_up = sum_terms(terms, expert_ids, w_gate.shape[0], scale)
    return hidden, token_grad, grad_gate, grad_up


def solution(mesh):
    both_axes = ("expert", "replica")
    in_specs = (
        P(both_axes, None),
        P(both_axes, None),
        P(None, both_axes, None),
        P(None, both_axes, None),
        P(),
    )
    out_specs = (
        P(both_axes, None),
        P(both_axes, None),
        P(None, both_axes, None),
        P(None, both_axes, None),
    )
    return jax.shard_map(
        per_device, mesh=mesh, in_specs=in_specs, out_specs=out_specs, check_vma=False
    )
```

time: 488 us -> 318 us (0.65)
  Pallas kernels: 0 us -> 299 us
  waiting for transfers between devices: 294 us -> 0 us
  blocking collectives: 73.5 us -> 0 us
  local copies, waits for them, and re-layouts: 48.6 us -> 10.6 us
  starting transfers between devices: 34.1 us -> 0 us
  matrix products: 27.4 us -> 0 us
    pallas_call x0 -> x3, Pallas kernels: none -> 299 us  [the longest x1 278 us: exchange(): pl.pallas_call(functools.partial(main_kernel, owners, members, chunks, ro...]
    all_to_all x7 -> x0, waiting for transfers between devices: 294 us -> none  [the longest x1 63.6 us: per_device(): lax.all_to_all(outgoing[1], 'replica', split_axis=0, concat_axis=0, tiled...]
    all_to_all x1 -> x0, blocking collectives: 73.5 us -> none  [per_device(): lax.all_to_all(outgoing[0], 'replica', split_axis=0, concat_axis=0, tiled...]
    all_to_all x7 -> x0, starting transfers between devices: 34.1 us -> none  [the longest x1 6.04 us: per_device(): lax.all_to_all(lax.all_to_all(part_gate, 'expert', split_axis=0, concat_a...]
    dot_general x8 -> x0, matrix products: 27.4 us -> none  [the longest x1 6.54 us: per_device(): up_pre = jnp.dot(tokens, up_whole, preferred_element_type=jnp.float32)]
    unnamed x36 -> x6, local copies, waits for them, and re-layouts: 19.1 us -> 2.21 us
    all_to_all x6 -> x0, local copies, waits for them, and re-layouts: 12.3 us -> none  [the longest x1 3.88 us: per_device(): lax.all_to_all(outgoing[0], 'replica', split_axis=0, concat_axis=0, tiled...]
    gather x2 -> x0, local copies, waits for them, and re-layouts: 6.86 us -> none  [pick_pieces(): jnp.take(weights, chosen, axis=0).reshape(leading + weights.shape[1:])]
  transfers between devices with their start and end apart: 7 -> 0, of which waited for: 7 -> 0; matrix products, arithmetic and copies ran while one was open for 12% -> 0% of each run, Pallas kernels for 0% -> 0%
where the time goes in v1:
time: 318 us; the launch traced here: 314 us
  Pallas kernels  299 us (94%)
  local copies, waits for them, and re-layouts  10.6 us (3%)
  other arithmetic  3.52 us (1%)
    pallas_call x1, Pallas kernels, exchange(): pl.pallas_call(functools.partial(main_kernel, owners, members, chunks, ro...  278 us
    pallas_call x1, Pallas kernels, sum_terms(): pl.pallas_call(functools.partial(sum_kernel, scale), grid=(chunks, rows /...  11.8 us
    pallas_call x1, Pallas kernels, pick(): pl.pallas_call(functools.partial(pick_kernel, step_blocks, chunks), grid_...  9.25 us
    convert_element_type x1, local copies, waits for them, and re-layouts, sum_terms(): spread = (selector[:, None, :, None] & unit[None, :, None, :]).astype(BF16)  8.42 us

profile of v1, /device:TPU:24, one launch (start us, length us, event | category | flops | bytes accessed | tf_op | source)
XLA Modules:
  0.0 314.0 jit_solution(1934425663859894290)
XLA Ops:
  0.6 0.7 iota_compare_fusion
  1.3 2.8 and_convert_fusion
  4.2 8.4 %reshape.44.spread_ref = bf16[512,512]{1,0:T(8,128)(2,1)} reshape(bf16[32,16,32,16]{3,2,1,0:T(8,128)(2,1)} %and_convert_fusion) | data formatting | bytes 1048576 | tf_op jit(solution)/shard_map/convert_element_type | solution.py:287
  12.6 9.2 %shard_map.84.out_w = bf16[3,32,64,512]{3,2,1,0:T(8,128)(2,1)} custom-call(s32[32]{0:T(128)} %ids_ref.1, bf16[32,64,768]{2,1,0:T(8,128)(2,1)} %gate_ref.1, bf16[32,64,768]{2,1,0:T(8,128)(2,1)} %up_ref.1), custom_call_target="tpu_custom_call" | custom-call | tf_op jit(solution)/shard_map/pallas_call | solution.py:49
  21.8 278.1 %shard_map.85 = (bf16[512,768]{1,0:T(8,128)(2,1)}, bf16[512,2048]{1,0:T(8,128)(2,1)}, bf16[3,32,64,512]{3,2,1,0:T(8,128)(2,1)}) custom-call(bf16[512,2048]{1,0:T(8,128)(2,1)} %tok_hbm.1, bf16[512,768]{1,0:T(8,128)(2,1)} %dh_hbm.1, bf16[3,32,64,512]{3,2,1,0:T(8,128)(2,1)} %shard_map.84.out_w), custom_call_target="tpu_custom_call" | custom-call | tf_op jit(solution)/shard_map/pallas_call | solution.py:239
  300.0 0.0 copy-start.1
  300.0 0.0 copy-start
  300.0 11.8 %shard_map.86 = (bf16[32,64,768]{2,1,0:T(8,128)(2,1)}, bf16[32,64,768]{2,1,0:T(8,128)(2,1)}) custom-call(bf16[512,512]{1,0:T(8,128)(2,1)} %reshape.44.spread_ref, bf16[3,32,64,512]{3,2,1,0:T(8,128)(2,1)} %get-tuple-element.11.terms_ref), custom_call_target="tpu_custom_call" | custom-call | tf_op jit(solution)/shard_map/pallas_call | solution.py:291
  311.8 0.0 copy-done.1
  311.8 0.9 copy.11
  312.7 0.0 copy-done
  312.7 1.3 copy.12
  (1 shorter events, 0.0 us)
Async XLA Ops:
  300.0 11.8 %copy-start.1 = (bf16[512,768]{1,0:T(8,128)(2,1)S(1)}, bf16[512,768]{1,0:T(8,128)(2,1)}, u32[]{:S(2)}) copy-start(bf16[512,768]{1,0:T(8,128)(2,1)} %get-tuple-element.18) | copy-start | bytes 2359300
  300.0 12.7 %copy-start = (bf16[512,2048]{1,0:T(8,128)(2,1)S(1)}, bf16[512,2048]{1,0:T(8,128)(2,1)}, u32[]{:S(2)}) copy-start(bf16[512,2048]{1,0:T(8,128)(2,1)} %get-tuple-element.19) | copy-start | bytes 6291460
